TPU v7x, 32 devices: a whole 2x2x4 slice. The times are simulated.
32 devices in a mesh: tm: 8 (over z, core), space: 4 (over y, x).
Axes of the slice: x: 2, y: 2, z: 4, core: 2. Of those that a mesh axis runs over, the one named last changes fastest.
Arguments:
- snapshots: bfloat16 [4096, 1024], P('space', 'tm'), may hold values from -23 to 23
- energy: bfloat16 [32, 7, 128, 128], P('space'), may hold values from -0.375 to 0.375
- neighbours: int32 [32, 7], P('space'), may hold values from 0 to 31, as said below
- sketch: float32 [3, 256, 128], replicated, may hold values from -0.375 to 0.375
Outputs:
- modes: bfloat16 [4, 8, 4096, 128], P(None, 'tm', 'space')
Inputs may be any that keep to these rules, and one draw needn't show every extreme that they name: `neighbours`: entry [b, k] lies within 2 blocks of b.
All inputs are finite; a program needn't handle non-finite values.
Results may differ from a plain program's by a relative error of at most 0.017.
Values may be sent and summed in bfloat16 or wider, within the bound.
No kernel may reach another device: no remote copies, remote signals or barrier semaphores. Data moves between devices by JAX's collectives and lax.ppermute only.
A program may use at most 64 MiB of HBM per device.

v0:
```python
import jax
import jax.numpy as jnp
from jax import lax
from jax.sharding import PartitionSpec as P

HB = 2


def padded_2(cells, sides, width):
    for axis, dim in sides:
        count = lax.axis_size(axis)
        ends = count - 1
        head = lax.slice_in_dim(cells, 0, width, axis=dim)
        tail = lax.slice_in_dim(cells, cells.shape[dim] - width, cells.shape[dim], axis=dim)
        cells = jnp.concatenate(
            [
                lax.ppermute(tail, axis, [(i, (i + 1) % count) for i in range(ends)]),
                cells,
                lax.ppermute(head, axis, [((i + 1) % count, i) for i in range(ends)]),
            ],
            axis=dim,
        )
    return cells


def from_partner(value, axis, bit):
    mask = 2**bit
    pairs = [(source, source ^ mask) for source in range(lax.axis_size(axis))]
    return lax.ppermute(value, axis, pairs)


def blocked(matrix_rows, block_rows):
    return matrix_rows.reshape(matrix_rows.shape[0] // block_rows, block_rows, matrix_rows.shape[1])


def image_of(padded, source, energy, local_index):
    block_rows = energy.shape[2]
    running = 3.0 * blocked(source, block_rows).astype(jnp.float32)
    for slot_index in range(energy.shape[1]):
        gathered = jnp.take(padded, local_index[:, slot_index], axis=0)
        running = running + jnp.einsum(
            "nij,njw->niw", energy[:, slot_index], gathered, preferred_element_type=jnp.float32
        )
    return running.astype(jnp.bfloat16).reshape(source.shape[0], source.shape[1])


def gram_of(energy_image):
    return jnp.einsum("rc,rd->cd", energy_image, energy_image, preferred_element_type=jnp.float32)


def side_by_side(upper_half, first, second, axis_number):
    return jnp.where(
        upper_half,
        jnp.concatenate([second, first], axis_number),
        jnp.concatenate([first, second], axis_number),
    )


def on_device(snapshots, energy, neighbours, sketch):
    block_rows = energy.shape[2]
    block_count = energy.shape[0]
    rows_dev = snapshots.shape[0]
    total_rows = rows_dev * lax.axis_size("space")
    first_block = lax.axis_index("space") * block_count - HB
    local_index = neighbours - first_block
    window_index = lax.axis_index("tm")
    highest = lax.Precision.HIGHEST
    padded = padded_2(blocked(snapshots, block_rows), (("space", 0),), HB)
    energy_image = image_of(padded, snapshots, energy, local_index)
    gram_matrix = lax.psum(gram_of(energy_image), "space") / total_rows
    lower_factor = jnp.linalg.cholesky(gram_matrix)
    identity = jnp.eye(snapshots.shape[1], dtype=jnp.float32)
    coefficients = jax.scipy.linalg.solve_triangular(lower_factor, identity, lower=True).T.astype(
        jnp.bfloat16
    )
    current = jnp.dot(snapshots, coefficients, preferred_element_type=jnp.float32).astype(
        jnp.bfloat16
    )
    images = jnp.dot(energy_image, coefficients, preferred_element_type=jnp.float32).astype(
        jnp.bfloat16
    )
    levels_kept = [current]
    for tree_level in range(sketch.shape[0]):
        upper_half = window_index // 2**tree_level % 2 == 1
        partner, partner_image = from_partner((current, images), "tm", tree_level)
        joined = side_by_side(upper_half, current, partner, 1)
        joined_image = side_by_side(upper_half, images, partner_image, 1)
        sketch_level = sketch[tree_level]
        gram_matrix = lax.psum(gram_of(joined_image), "space") / total_rows
        columns = jnp.dot(gram_matrix, sketch_level, precision=highest)
        inner_gram = jnp.dot(
            columns.T, jnp.dot(gram_matrix, columns, precision=highest), precision=highest
        )
        lower_factor = jnp.linalg.cholesky(inner_gram)
        coefficients = jax.scipy.linalg.solve_triangular(
            lower_factor, columns.T, lower=True
        ).T.astype(jnp.bfloat16)
        new_modes = jnp.dot(joined, coefficients, preferred_element_type=jnp.float32).astype(
            jnp.bfloat16
        )
        new_image = jnp.dot(joined_image, coefficients, preferred_element_type=jnp.float32).astype(
            jnp.bfloat16
        )
        current = new_modes
        images = new_image
        levels_kept.append(current)
    return jnp.stack(levels_kept)[:, None]


def solution(mesh):
    placed = (P("space", "tm"), P("space", None, None, None), P("space", None), P())
    return jax.shard_map(
        on_device,
        mesh=mesh,
        in_specs=placed,
        out_specs=P(None, "tm", "space", None),
        check_vma=False,
    )
```

profile of v0, /device:TPU:0, one launch (start us, length us, event | category | flops | bytes accessed | tf_op | source)
XLA Modules:
  0.0 343.3 jit_solution(3305505052904443484)
XLA Ops:
  8.7 5.5 %collective-permute-start = (bf16[2,128,128]{2,1,0:T(8,128)(2,1)S(1)}, bf16[2,128,128]{2,1,0:T(8,128)(2,1)S(1)}, u32[]{:S(2)}, u32[]{:S(2)}) collective-permute-start(bf16[2,128,128]{2,1,0:T(8,128)(2,1)S(1)} %bitcast.162), channel_id=1, source_target_pairs={{0,1},{1,2},{2,3},{4,5},{5,6},{6,7},{8,9},{9,10},{10,11},{12,13},{... | collective-permute-start | bytes 196616 | tf_op jit(solution)/shard_map/ppermute | solution.py:17
  29.1 44.5 %all-reduce.5.cloned.1.call-done = f32[128,128]{0,1:T(8,128)} async-done(((f32[128,128]{0,1:T(8,128)}), f32[128,128]{0,1:T(8,128)}) %all-reduce.5.cloned.1.call-update) | async-done | bytes 65552 | tf_op jit(solution)/shard_map/psum | solution.py:70
  75.4 11.7 %cholesky.74 = f32[128,128]{1,0:T(8,128)S(1)} custom-call(f32[128,128]{1,0:T(8,128)S(1)} %fusion.109), custom_call_target="Cholesky" | custom-call | tf_op jit(solution)/shard_map/jit(cholesky)/cholesky | solution.py:71
  88.4 9.8 %custom-call.9 = f32[1,128,128]{1,2,0:T(8,128)S(1)} custom-call(f32[1,128,128]{2,1,0:T(8,128)S(1)} %fusion.98), custom_call_target="InvertDiagBlocksLowerTriangular" | custom-call | tf_op jit(solution)/shard_map/jit(_solve_triangular)/triangular_solve | solution.py:73
  98.9 1.5 collective-permute-done.3
  101.8 43.0 %all-reduce.7.cloned.1.call-done = f32[256,256]{1,0:T(8,128)} async-done(((f32[256,256]{1,0:T(8,128)}), f32[256,256]{1,0:T(8,128)}) %all-reduce.7.cloned.1.call-update) | async-done | bytes 262160 | tf_op jit(solution)/shard_map/psum | solution.py:89
  144.7 1.3 fusion.72
  146.1 1.3 fusion.70
  147.9 11.7 %cholesky.85 = f32[128,128]{1,0:T(8,128)S(1)} custom-call(f32[128,128]{1,0:T(8,128)S(1)} %fusion.107), custom_call_target="Cholesky" | custom-call | tf_op jit(solution)/shard_map/jit(cholesky)/cholesky | solution.py:94
  161.0 9.8 %custom-call.12 = f32[1,128,128]{1,2,0:T(8,128)S(1)} custom-call(f32[1,128,128]{2,1,0:T(8,128)S(1)} %fusion.99), custom_call_target="InvertDiagBlocksLowerTriangular" | custom-call | tf_op jit(solution)/shard_map/jit(_solve_triangular)/triangular_solve | solution.py:95
  171.4 1.6 collective-permute-start.5
  172.9 6.1 %collective-permute-done.5 = bf16[1024,128]{0,1:T(8,128)(2,1)S(1)} collective-permute-done((bf16[1024,128]{0,1:T(8,128)(2,1)S(1)}, bf16[1024,128]{0,1:T(8,128)(2,1)S(1)}, u32[]{:S(2)}, u32[]{:S(2)}) %collective-permute-start.5) | collective-permute-done | bytes 262176 | tf_op jit(solution)/shard_map/ppermute | solution.py:29
  180.8 42.6 %all-reduce.9.cloned.1.call-done = f32[256,256]{1,0:T(8,128)} async-done(((f32[256,256]{1,0:T(8,128)}), f32[256,256]{1,0:T(8,128)}) %all-reduce.9.cloned.1.call-update) | async-done | bytes 262160 | tf_op jit(solution)/shard_map/psum | solution.py:89
  224.7 1.3 fusion.66
  226.5 11.7 %cholesky.96 = f32[128,128]{1,0:T(8,128)S(1)} custom-call(f32[128,128]{1,0:T(8,128)S(1)} %fusion.105), custom_call_target="Cholesky" | custom-call | tf_op jit(solution)/shard_map/jit(cholesky)/cholesky | solution.py:94
  239.6 9.8 %custom-call.13 = f32[1,128,128]{1,2,0:T(8,128)S(1)} custom-call(f32[1,128,128]{2,1,0:T(8,128)S(1)} %fusion.100), custom_call_target="InvertDiagBlocksLowerTriangular" | custom-call | tf_op jit(solution)/shard_map/jit(_solve_triangular)/triangular_solve | solution.py:95
  250.0 2.5 collective-permute-start.7
  252.8 1.6 collective-permute-start.4
  254.3 9.9 %collective-permute-done.7 = bf16[1024,128]{0,1:T(8,128)(2,1)S(1)} collective-permute-done((bf16[1024,128]{0,1:T(8,128)(2,1)S(1)}, bf16[1024,128]{0,1:T(8,128)(2,1)S(1)}, u32[]{:S(2)}, u32[]{:S(2)}) %collective-permute-start.7) | collective-permute-done | bytes 262176 | tf_op jit(solution)/shard_map/ppermute | solution.py:29
  266.0 42.4 %all-reduce.11.cloned.1.call-done = f32[256,256]{1,0:T(8,128)} async-done(((f32[256,256]{1,0:T(8,128)}), f32[256,256]{1,0:T(8,128)}) %all-reduce.11.cloned.1.call-update) | async-done | bytes 262160 | tf_op jit(solution)/shard_map/psum | solution.py:89
  308.4 1.3 fusion.64
  309.8 1.3 fusion.62
  311.6 12.0 %cholesky.107 = f32[128,128]{1,0:T(8,128)S(1)} custom-call(f32[128,128]{1,0:T(8,128)S(1)} %fusion.103), custom_call_target="Cholesky" | custom-call | tf_op jit(solution)/shard_map/jit(cholesky)/cholesky | solution.py:94
  324.9 9.8 %custom-call.14 = f32[1,128,128]{1,2,0:T(8,128)S(1)} custom-call(f32[1,128,128]{2,1,0:T(8,128)S(1)} %fusion.101), custom_call_target="InvertDiagBlocksLowerTriangular" | custom-call | tf_op jit(solution)/shard_map/jit(_solve_triangular)/triangular_solve | solution.py:95
  (102 shorter events, 35.7 us)
Async XLA Ops:
  6.5 67.0 %all-reduce.5.cloned.1.call-start = ((), (), s32[]{:S(2)}) async-start(), calls=%async_computation | async-start | bytes 131072 | tf_op jit(solution)/shard_map/psum | solution.py:70
  7.4 9.6 %collective-permute-start.1 = (bf16[2,128,128]{2,1,0:T(8,128)(2,1)S(1)}, bf16[2,128,128]{2,1,0:T(8,128)(2,1)S(1)}, u32[]{:S(2)}, u32[]{:S(2)}) collective-permute-start(bf16[2,128,128]{2,1,0:T(8,128)(2,1)S(1)} %bitcast.163), channel_id=1, source_target_pairs={{1,0},{2,1},{3,2},{5,4},{6,5},{7,6},{9,8},{10,9},{11,10},{13,12},{... | collective-permute-start | bytes 196616 | tf_op jit(solution)/shard_map/ppermute | solution.py:19
  8.7 8.3 %collective-permute-start = (bf16[2,128,128]{2,1,0:T(8,128)(2,1)S(1)}, bf16[2,128,128]{2,1,0:T(8,128)(2,1)S(1)}, u32[]{:S(2)}, u32[]{:S(2)}) collective-permute-start(bf16[2,128,128]{2,1,0:T(8,128)(2,1)S(1)} %bitcast.162), channel_id=1, source_target_pairs={{0,1},{1,2},{2,3},{4,5},{5,6},{6,7},{8,9},{9,10},{10,11},{12,13},{... | collective-permute-start | bytes 196616 | tf_op jit(solution)/shard_map/ppermute | solution.py:17
  18.1 5.6 %copy-start.1 = (bf16[8,7,128,128]{3,2,1,0:T(8,128)(2,1)S(1)}, bf16[8,7,128,128]{3,2,1,0:T(8,128)(2,1)}, u32[]{:S(2)}) copy-start(bf16[8,7,128,128]{3,2,1,0:T(8,128)(2,1)} %param.10) | copy-start | bytes 5505028
  23.7 2.2 copy-start.2
  26.8 1.0 copy-start
  26.8 0.9 copy-start.4
  29.0 115.7 %all-reduce.7.cloned.1.call-start = ((), (), s32[]{:S(2)}) async-start(), calls=%async_computation.1 | async-start | bytes 524288 | tf_op jit(solution)/shard_map/psum | solution.py:89
  87.1 57.6 %copy-start.3 = (f32[3,256,128]{2,1,0:T(8,128)S(1)}, f32[3,256,128]{2,1,0:T(8,128)}, u32[]{:S(2)}) copy-start(f32[3,256,128]{2,1,0:T(8,128)} %param.12) | copy-start | bytes 1179652
  98.8 1.6 collective-permute-start.3
  101.5 121.8 %all-reduce.9.cloned.1.call-start = ((), (), s32[]{:S(2)}) async-start(), calls=%async_computation.2 | async-start | bytes 524288 | tf_op jit(solution)/shard_map/psum | solution.py:89
  171.4 7.6 %collective-permute-start.5 = (bf16[1024,128]{0,1:T(8,128)(2,1)S(1)}, bf16[1024,128]{0,1:T(8,128)(2,1)S(1)}, u32[]{:S(2)}, u32[]{:S(2)}) collective-permute-start(bf16[1024,128]{0,1:T(8,128)(2,1)S(1)} %convolution_convert_fusion.3), channel_id=1, source_target_pairs={{0,8},{4,12},{8,0},{12,4},{16,24},{20,28},{24,16},{28,20},{1,9},{5... | collective-permute-start | bytes 786440 | tf_op jit(solution)/shard_map/ppermute | solution.py:29
  180.2 128.3 %all-reduce.11.cloned.1.call-start = ((), (), s32[]{:S(2)}) async-start(), calls=%async_computation.3 | async-start | bytes 524288 | tf_op jit(solution)/shard_map/psum | solution.py:89
  180.7 71.8 %collective-permute-start.2 = (bf16[1024,128]{0,1:T(8,128)(2,1)S(1)}, bf16[1024,128]{0,1:T(8,128)(2,1)S(1)}, u32[]{:S(2)}, u32[]{:S(2)}) collective-permute-start(bf16[1024,128]{0,1:T(8,128)(2,1)S(1)} %bitcast.157), channel_id=1, source_target_pairs={{0,4},{4,0},{8,12},{12,8},{16,20},{20,16},{24,28},{28,24},{1,5},{5... | collective-permute-start | bytes 786440 | tf_op jit(solution)/shard_map/ppermute | solution.py:29
  250.0 14.3 %collective-permute-start.7 = (bf16[1024,128]{0,1:T(8,128)(2,1)S(1)}, bf16[1024,128]{0,1:T(8,128)(2,1)S(1)}, u32[]{:S(2)}, u32[]{:S(2)}) collective-permute-start(bf16[1024,128]{0,1:T(8,128)(2,1)S(1)} %convolution_convert_fusion.1), channel_id=1, source_target_pairs={{0,16},{4,20},{8,24},{12,28},{16,0},{20,4},{24,8},{28,12},{1,17},{... | collective-permute-start | bytes 786440 | tf_op jit(solution)/shard_map/ppermute | solution.py:29
  252.8 12.6 %collective-permute-start.4 = (bf16[1024,128]{0,1:T(8,128)(2,1)S(1)}, bf16[1024,128]{0,1:T(8,128)(2,1)S(1)}, u32[]{:S(2)}, u32[]{:S(2)}) collective-permute-start(bf16[1024,128]{0,1:T(8,128)(2,1)S(1)} %convolution_convert_fusion.4), channel_id=1, source_target_pairs={{0,8},{4,12},{8,0},{12,4},{16,24},{20,28},{24,16},{28,20},{1,9},{5... | collective-permute-start | bytes 786440 | tf_op jit(solution)/shard_map/ppermute | solution.py:29
  265.7 69.4 %collective-permute-start.6 = (bf16[1024,128]{0,1:T(8,128)(2,1)S(1)}, bf16[1024,128]{0,1:T(8,128)(2,1)S(1)}, u32[]{:S(2)}, u32[]{:S(2)}) collective-permute-start(bf16[1024,128]{0,1:T(8,128)(2,1)S(1)} %convolution_convert_fusion.2), channel_id=1, source_target_pairs={{0,16},{4,20},{8,24},{12,28},{16,0},{20,4},{24,8},{28,12},{1,17},{... | collective-permute-start | bytes 786440 | tf_op jit(solution)/shard_map/ppermute | solution.py:29
Sparse Core Ops, SparseCore 0:
  29.2 44.3 all-reduce.4
  101.7 43.0 all-reduce.6
  180.3 43.0 all-reduce.8
  265.5 42.9 all-reduce.10
where the time goes:
time: 344 us; the launch traced here: 343 us
  waiting for transfers between devices  190 us (55%)
  other arithmetic  97 us (28%)
  matrix products  20.8 us (6%)
  between operations  13.7 us (4%)
  starting transfers between devices  13.4 us (4%)
  local copies, waits for them, and re-layouts  8.4 us (2%)
    psum x3, waiting for transfers between devices, on_device(): gram_matrix = lax.psum(gram_of(joined_image), 'space') / total_rows  128 us
    psum x1, waiting for transfers between devices, on_device(): gram_matrix = lax.psum(gram_of(energy_image), 'space') / total_rows  44.5 us
    another operation x9, other arithmetic, on_device(): lower_factor = jnp.linalg.cholesky(inner_gram)  37.4 us
    another operation x6, other arithmetic, on_device(): jax.scipy.linalg.solve_triangular(lower_factor, columns.T, lower=True)  31.4 us
    ppermute x6, waiting for transfers between devices, from_partner(): return lax.ppermute(value, axis, pairs)  17.5 us
    another operation x3, other arithmetic, on_device(): lower_factor = jnp.linalg.cholesky(gram_matrix)  12.4 us
    another operation x2, other arithmetic, on_device(): jax.scipy.linalg.solve_triangular(lower_factor, identity, lower=True)  10.5 us
  transfers between devices with their start and end apart: 12, of which 7 were waited for; matrix products, arithmetic and copies ran while one was open for 17% of the time, Pallas kernels for 0%

commit v1 on v0

--- a/solution.py
+++ b/solution.py
@@ -86,7 +86,7 @@
         joined = side_by_side(upper_half, current, partner, 1)
         joined_image = side_by_side(upper_half, images, partner_image, 1)
         sketch_level = sketch[tree_level]
-        gram_matrix = lax.psum(gram_of(joined_image), "space") / total_rows
+        gram_matrix = jnp.sum(lax.all_gather(gram_of(joined_image), "space"), axis=0) / total_rows
         columns = jnp.dot(gram_matrix, sketch_level, precision=highest)
         inner_gram = jnp.dot(
             columns.T, jnp.dot(gram_matrix, columns, precision=highest), precision=highest

time: 344 us -> 294 us (0.85)
  waiting for transfers between devices: 190 us -> 141 us
  matrix products: 20.8 us -> 14.9 us
    psum x3 -> x0, waiting for transfers between devices: 128 us -> none  [on_device(): gram_matrix = lax.psum(gram_of(joined_image), 'space') / total_rows]
    all_gather x0 -> x3, waiting for transfers between devices: none -> 66.4 us  [on_device(): lax.all_gather(gram_of(joined_image), 'space')]
    ppermute x6, waiting for transfers between devices: 17.5 us -> 29.3 us  [from_partner(): return lax.ppermute(value, axis, pairs)]
    reduce_sum x0 -> x3, other arithmetic: none -> 3.96 us  [on_device(): jnp.sum(lax.all_gather(gram_of(joined_image), 'space'), axis=0) / total_rows]
  transfers between devices with their start and end apart: 12 -> 12, of which waited for: 7 -> 9; matrix products, arithmetic and copies ran while one was open for 17% -> 10% of each run, Pallas kernels for 0% -> 0%
where the time goes in v1:
time: 294 us; the launch traced here: 293 us
  waiting for transfers between devices  141 us (48%)
  other arithmetic  100 us (34%)
  matrix products  14.9 us (5%)
  starting transfers between devices  14.2 us (5%)
  between operations  13.7 us (5%)
  local copies, waits for them, and re-layouts  9.08 us (3%)
    all_gather x3, waiting for transfers between devices, on_device(): lax.all_gather(gram_of(joined_image), 'space')  66.4 us
    psum x1, waiting for transfers between devices, on_device(): gram_matrix = lax.psum(gram_of(energy_image), 'space') / total_rows  45 us
    another operation x9, other arithmetic, on_device(): lower_factor = jnp.linalg.cholesky(inner_gram)  37.4 us
    another operation x6, other arithmetic, on_device(): jax.scipy.linalg.solve_triangular(lower_factor, columns.T, lower=True)  31.4 us
    ppermute x6, waiting for transfers between devices, from_partner(): return lax.ppermute(value, axis, pairs)  29.3 us
    another operation x3, other arithmetic, on_device(): lower_factor = jnp.linalg.cholesky(gram_matrix)  12.4 us
    another operation x2, other arithmetic, on_device(): jax.scipy.linalg.solve_triangular(lower_factor, identity, lower=True)  10.5 us
    ppermute x6, starting transfers between devices, from_partner(): return lax.ppermute(value, axis, pairs)  6.91 us
  transfers between devices with their start and end apart: 12, of which 9 were waited for; matrix products, arithmetic and copies ran while one was open for 10% of the time, Pallas kernels for 0%

profile of v1, /device:TPU:0, one launch (start us, length us, event | category | flops | bytes accessed | tf_op | source)
XLA Modules:
  0.0 293.1 jit_solution(14254848844361291021)
XLA Ops:
  8.7 5.5 %collective-permute-start = (bf16[2,128,128]{2,1,0:T(8,128)(2,1)S(1)}, bf16[2,128,128]{2,1,0:T(8,128)(2,1)S(1)}, u32[]{:S(2)}, u32[]{:S(2)}) collective-permute-start(bf16[2,128,128]{2,1,0:T(8,128)(2,1)S(1)} %bitcast.168), channel_id=1, source_target_pairs={{0,1},{1,2},{2,3},{4,5},{5,6},{6,7},{8,9},{9,10},{10,11},{12,13},{... | collective-permute-start | bytes 196616 | tf_op jit(solution)/shard_map/ppermute | solution.py:17
  29.0 45.0 %all-reduce.2.cloned.1.call-done = f32[128,128]{0,1:T(8,128)} async-done(((f32[128,128]{0,1:T(8,128)}), f32[128,128]{0,1:T(8,128)}) %all-reduce.2.cloned.1.call-update) | async-done | bytes 65552 | tf_op jit(solution)/shard_map/psum | solution.py:70
  75.8 11.7 %cholesky.74 = f32[128,128]{1,0:T(8,128)S(1)} custom-call(f32[128,128]{1,0:T(8,128)S(1)} %fusion.109), custom_call_target="Cholesky" | custom-call | tf_op jit(solution)/shard_map/jit(cholesky)/cholesky | solution.py:71
  88.9 9.8 %custom-call.9 = f32[1,128,128]{1,2,0:T(8,128)S(1)} custom-call(f32[1,128,128]{2,1,0:T(8,128)S(1)} %fusion.98), custom_call_target="InvertDiagBlocksLowerTriangular" | custom-call | tf_op jit(solution)/shard_map/jit(_solve_triangular)/triangular_solve | solution.py:73
  99.3 1.5 collective-permute-done.3
  102.2 26.4 %all-gather.7.cloned.1.call-done = f32[1024,256]{1,0:T(8,128)} async-done(((f32[256,256]{1,0:T(8,128)}), f32[1024,256]{1,0:T(8,128)}) %all-gather.7.cloned.1.call-update) | async-done | bytes 1048592 | tf_op jit(solution)/shard_map/all_gather | solution.py:89
  128.6 1.3 reduce_sum.27
  131.2 11.7 %cholesky.85 = f32[128,128]{1,0:T(8,128)S(1)} custom-call(f32[128,128]{1,0:T(8,128)S(1)} %fusion.107), custom_call_target="Cholesky" | custom-call | tf_op jit(solution)/shard_map/jit(cholesky)/cholesky | solution.py:94
  144.3 9.8 %custom-call.12 = f32[1,128,128]{1,2,0:T(8,128)S(1)} custom-call(f32[1,128,128]{2,1,0:T(8,128)S(1)} %fusion.99), custom_call_target="InvertDiagBlocksLowerTriangular" | custom-call | tf_op jit(solution)/shard_map/jit(_solve_triangular)/triangular_solve | solution.py:95
  154.7 1.5 collective-permute-start.5
  156.2 6.4 %collective-permute-done.5 = bf16[1024,128]{0,1:T(8,128)(2,1)S(1)} collective-permute-done((bf16[1024,128]{0,1:T(8,128)(2,1)S(1)}, bf16[1024,128]{0,1:T(8,128)(2,1)S(1)}, u32[]{:S(2)}, u32[]{:S(2)}) %collective-permute-start.5) | collective-permute-done | bytes 262176 | tf_op jit(solution)/shard_map/ppermute | solution.py:29
  164.1 26.4 %all-gather.9.cloned.1.call-done = f32[1024,256]{1,0:T(8,128)} async-done(((f32[256,256]{1,0:T(8,128)}), f32[1024,256]{1,0:T(8,128)}) %all-gather.9.cloned.1.call-update) | async-done | bytes 1048592 | tf_op jit(solution)/shard_map/all_gather | solution.py:89
  190.4 1.3 reduce_sum.28
  193.0 11.7 %cholesky.96 = f32[128,128]{1,0:T(8,128)S(1)} custom-call(f32[128,128]{1,0:T(8,128)S(1)} %fusion.105), custom_call_target="Cholesky" | custom-call | tf_op jit(solution)/shard_map/jit(cholesky)/cholesky | solution.py:94
  206.1 9.8 %custom-call.13 = f32[1,128,128]{1,2,0:T(8,128)S(1)} custom-call(f32[1,128,128]{2,1,0:T(8,128)S(1)} %fusion.100), custom_call_target="InvertDiagBlocksLowerTriangular" | custom-call | tf_op jit(solution)/shard_map/jit(_solve_triangular)/triangular_solve | solution.py:95
  216.5 2.5 collective-permute-start.7
  219.0 12.0 %collective-permute-done.7 = bf16[1024,128]{0,1:T(8,128)(2,1)S(1)} collective-permute-done((bf16[1024,128]{0,1:T(8,128)(2,1)S(1)}, bf16[1024,128]{0,1:T(8,128)(2,1)S(1)}, u32[]{:S(2)}, u32[]{:S(2)}) %collective-permute-start.7) | collective-permute-done | bytes 262176 | tf_op jit(solution)/shard_map/ppermute | solution.py:29
  232.4 1.5 collective-permute-done.2
  234.8 7.9 %collective-permute-done.4 = bf16[1024,128]{0,1:T(8,128)(2,1)S(1)} collective-permute-done((bf16[1024,128]{0,1:T(8,128)(2,1)S(1)}, bf16[1024,128]{0,1:T(8,128)(2,1)S(1)}, u32[]{:S(2)}, u32[]{:S(2)}) %collective-permute-start.4) | collective-permute-done | bytes 262176 | tf_op jit(solution)/shard_map/ppermute | solution.py:29
  243.0 2.2 collective-permute-start.6
  245.2 13.6 %all-gather.11.cloned.1.call-done = f32[1024,256]{1,0:T(8,128)} async-done(((f32[256,256]{1,0:T(8,128)}), f32[1024,256]{1,0:T(8,128)}) %all-gather.11.cloned.1.call-update) | async-done | bytes 1048592 | tf_op jit(solution)/shard_map/all_gather | solution.py:89
  258.8 1.3 reduce_sum.29
  261.3 11.9 %cholesky.107 = f32[128,128]{1,0:T(8,128)S(1)} custom-call(f32[128,128]{1,0:T(8,128)S(1)} %fusion.103), custom_call_target="Cholesky" | custom-call | tf_op jit(solution)/shard_map/jit(cholesky)/cholesky | solution.py:94
  274.6 9.8 %custom-call.14 = f32[1,128,128]{1,2,0:T(8,128)S(1)} custom-call(f32[1,128,128]{2,1,0:T(8,128)S(1)} %fusion.101), custom_call_target="InvertDiagBlocksLowerTriangular" | custom-call | tf_op jit(solution)/shard_map/jit(_solve_triangular)/triangular_solve | solution.py:95
  (105 shorter events, 36.8 us)
Async XLA Ops:
  6.5 67.5 %all-reduce.2.cloned.1.call-start = ((), (), s32[]{:S(2)}) async-start(), calls=%async_computation | async-start | bytes 131072 | tf_op jit(solution)/shard_map/psum | solution.py:70
  7.4 9.1 %collective-permute-start.1 = (bf16[2,128,128]{2,1,0:T(8,128)(2,1)S(1)}, bf16[2,128,128]{2,1,0:T(8,128)(2,1)S(1)}, u32[]{:S(2)}, u32[]{:S(2)}) collective-permute-start(bf16[2,128,128]{2,1,0:T(8,128)(2,1)S(1)} %bitcast.169), channel_id=1, source_target_pairs={{1,0},{2,1},{3,2},{5,4},{6,5},{7,6},{9,8},{10,9},{11,10},{13,12},{... | collective-permute-start | bytes 196616 | tf_op jit(solution)/shard_map/ppermute | solution.py:19
  8.7 7.8 %collective-permute-start = (bf16[2,128,128]{2,1,0:T(8,128)(2,1)S(1)}, bf16[2,128,128]{2,1,0:T(8,128)(2,1)S(1)}, u32[]{:S(2)}, u32[]{:S(2)}) collective-permute-start(bf16[2,128,128]{2,1,0:T(8,128)(2,1)S(1)} %bitcast.168), channel_id=1, source_target_pairs={{0,1},{1,2},{2,3},{4,5},{5,6},{6,7},{8,9},{9,10},{10,11},{12,13},{... | collective-permute-start | bytes 196616 | tf_op jit(solution)/shard_map/ppermute | solution.py:17
  17.6 6.3 %copy-start.1 = (bf16[8,7,128,128]{3,2,1,0:T(8,128)(2,1)S(1)}, bf16[8,7,128,128]{3,2,1,0:T(8,128)(2,1)}, u32[]{:S(2)}) copy-start(bf16[8,7,128,128]{3,2,1,0:T(8,128)(2,1)} %param.10) | copy-start | bytes 5505028
  23.8 2.6 copy-start.2
  26.7 1.0 copy-start
  26.7 0.9 copy-start.4
  29.0 99.6 %all-gather.7.cloned.1.call-start = ((), (), s32[]{:S(2)}) async-start(), calls=%async_computation.1 | async-start | bytes 1310720 | tf_op jit(solution)/shard_map/all_gather | solution.py:89
  99.2 1.6 collective-permute-start.3
  99.3 30.6 %copy-start.3 = (f32[3,256,128]{2,1,0:T(8,128)S(1)}, f32[3,256,128]{2,1,0:T(8,128)}, u32[]{:S(2)}) copy-start(f32[3,256,128]{2,1,0:T(8,128)} %param.12) | copy-start | bytes 1179652
  102.0 88.5 %all-gather.9.cloned.1.call-start = ((), (), s32[]{:S(2)}) async-start(), calls=%async_computation.2 | async-start | bytes 1310720 | tf_op jit(solution)/shard_map/all_gather | solution.py:89
  154.7 7.9 %collective-permute-start.5 = (bf16[1024,128]{0,1:T(8,128)(2,1)S(1)}, bf16[1024,128]{0,1:T(8,128)(2,1)S(1)}, u32[]{:S(2)}, u32[]{:S(2)}) collective-permute-start(bf16[1024,128]{0,1:T(8,128)(2,1)S(1)} %convolution_convert_fusion.3), channel_id=1, source_target_pairs={{0,8},{4,12},{8,0},{12,4},{16,24},{20,28},{24,16},{28,20},{1,9},{5... | collective-permute-start | bytes 786440 | tf_op jit(solution)/shard_map/ppermute | solution.py:29
  163.8 95.0 %all-gather.11.cloned.1.call-start = ((), (), s32[]{:S(2)}) async-start(), calls=%async_computation.3 | async-start | bytes 1310720 | tf_op jit(solution)/shard_map/all_gather | solution.py:89
  216.5 14.4 %collective-permute-start.7 = (bf16[1024,128]{0,1:T(8,128)(2,1)S(1)}, bf16[1024,128]{0,1:T(8,128)(2,1)S(1)}, u32[]{:S(2)}, u32[]{:S(2)}) collective-permute-start(bf16[1024,128]{0,1:T(8,128)(2,1)S(1)} %convolution_convert_fusion.1), channel_id=1, source_target_pairs={{0,16},{4,20},{8,24},{12,28},{16,0},{20,4},{24,8},{28,12},{1,17},{... | collective-permute-start | bytes 786440 | tf_op jit(solution)/shard_map/ppermute | solution.py:29
  232.4 1.6 collective-permute-start.2
  234.3 8.4 %collective-permute-start.4 = (bf16[1024,128]{0,1:T(8,128)(2,1)S(1)}, bf16[1024,128]{0,1:T(8,128)(2,1)S(1)}, u32[]{:S(2)}, u32[]{:S(2)}) collective-permute-start(bf16[1024,128]{0,1:T(8,128)(2,1)S(1)} %convolution_convert_fusion.4), channel_id=1, source_target_pairs={{0,8},{4,12},{8,0},{12,4},{16,24},{20,28},{24,16},{28,20},{1,9},{5... | collective-permute-start | bytes 786440 | tf_op jit(solution)/shard_map/ppermute | solution.py:29
  243.0 41.8 %collective-permute-start.6 = (bf16[1024,128]{0,1:T(8,128)(2,1)S(1)}, bf16[1024,128]{0,1:T(8,128)(2,1)S(1)}, u32[]{:S(2)}, u32[]{:S(2)}) collective-permute-start(bf16[1024,128]{0,1:T(8,128)(2,1)S(1)} %convolution_convert_fusion.2), channel_id=1, source_target_pairs={{0,16},{4,20},{8,24},{12,28},{16,0},{20,4},{24,8},{28,12},{1,17},{... | collective-permute-start | bytes 786440 | tf_op jit(solution)/shard_map/ppermute | solution.py:29
Sparse Core Ops, SparseCore 0:
  29.1 44.8 all-reduce.1
  102.1 26.4 all-gather.6
  163.9 26.4 all-gather.8
  232.2 26.4 all-gather.10
